TPU v7x, 512 devices: a whole 4x4x16 slice. The times are simulated.
512 devices in a mesh: lon: 32 (over x, z_lo), lat: 16 (over y, z_hi, core).
Axes of the slice: x: 4, y: 4, z: 16 (z_hi: 2, z_lo: 8; z = z_hi * 8 + z_lo), core: 2. Of those that a mesh axis runs over, the one named last changes fastest.
Arguments:
- increment: bfloat16 [2, 127, 128, 4096], P(None, None, 'lat', 'lon'), may hold values from -6 to 6
- std_dev: bfloat16 [2, 127, 128, 4096], P(None, None, 'lat', 'lon'), may hold values from 0.5 to 4
- level_group: int32 [127], replicated, may hold values from 0 to 3, never falling along the last dimension, each value on 1 to 40 neighbouring positions
- lon_reach: float32 [2, 4, 4], replicated, may hold values from 8 to 16384
- lon_weight: float32 [2, 4, 4], replicated, may hold values from 0.2 to 1
- lat_reach: float32 [2, 4, 4], replicated, may hold values from 2 to 512
- lat_weight: float32 [2, 4, 4], replicated, may hold values from 0.2 to 1
- vertical: float32 [2, 127, 127], replicated, may hold values from -0.5 to 0.5
Outputs:
- covaried: bfloat16 [2, 127, 128, 4096], P(None, None, 'lat', 'lon')
Inputs may be any that keep to these rules, and one draw needn't show every extreme that they name: level_group never falls along the levels; each of the 4 groups holds 1 to 40 consecutive levels and one holds exactly 40.
All inputs are finite; a program needn't handle non-finite values.
Results may differ from a plain program's by a relative error of at most 0.003.
Values sent between devices are 32-bit elements; how exact they have to be, the bound alone decides.
A program may use at most 64 MiB of HBM per device.

v0:
```python
import jax
import jax.numpy as jnp
from jax import lax
from jax.sharding import PartitionSpec as P

MOST = 40


def prefix_2(part, axis, combine, identity, reverse):
    count = lax.axis_size(axis)
    place = lax.axis_index(axis)
    ahead = count - 1 - place if reverse else place
    gathered = jax.tree.map(lambda a: lax.all_gather(a, axis), part)
    state = jax.tree.map(lambda a, e: jnp.zeros_like(a) + jnp.asarray(e, a.dtype), part, identity)

    def one(step, state):
        source = count - 1 - step if reverse else step
        return combine(
            state, jax.tree.map(lambda a: lax.dynamic_index_in_dim(a, source, 0, False), gathered)
        )

    return lax.fori_loop(0, ahead, one, state)


def from_root(value, axis, source):
    kept = jnp.where(lax.axis_index(axis) == source, value, 0).astype(value.dtype)
    return lax.psum(kept, axis)


def level_values(onehot, grouped):
    return jnp.einsum("kg,vgp->vkp", onehot, grouped, precision=lax.Precision.HIGHEST)


def toeplitz_tables(inverse_group, weights_group, length):
    indices = jnp.arange(length)
    spacing = (indices[None, :] - indices[:, None]).astype(jnp.float32)
    rates = jnp.exp(-jnp.maximum(spacing, 0.0) * inverse_group[..., None, None])
    terms = jnp.sum(weights_group[..., None, None] * rates, axis=2)
    return jnp.where(spacing >= 0.0, terms, 0.0)


def grouped_product(current, blocks, level_group, pattern):
    levels = current.shape[1]
    result = jnp.zeros_like(current)
    for group in range(blocks.shape[1]):
        first_level = jnp.minimum(jnp.sum((level_group < group).astype(jnp.int32)), levels - MOST)
        window = lax.dynamic_slice_in_dim(current, first_level, MOST, 1)
        product = jnp.einsum(pattern, window, blocks[:, group], precision=lax.Precision.HIGHEST)
        labels = lax.dynamic_slice_in_dim(level_group, first_level, MOST, 0)
        member_mask = (labels == group)[None, :, None, None]
        previous = lax.dynamic_slice_in_dim(result, first_level, MOST, 1)
        result = lax.dynamic_update_slice_in_dim(
            result, previous + jnp.where(member_mask, product, 0.0), first_level, 1
        )
    return result


def affine_join(earlier, later):
    return (earlier[0] * later[0], later[0] * earlier[1] + later[1])


def cycle_carry(edge_sums, inverse_level, length, reverse):
    members = lax.axis_size("lon")
    inverse = jnp.transpose(inverse_level, (2, 0, 1))[..., None]
    closure = 1.0 - jnp.exp(-(members * length) * inverse)
    stride = jnp.exp(-length * inverse)
    factor, prefix = prefix_2(
        (stride, edge_sums),
        "lon",
        affine_join,
        (jnp.ones_like(stride), jnp.zeros_like(edge_sums)),
        reverse,
    )
    leaving = stride * prefix + edge_sums
    anchor = 0 if reverse else members - 1
    beside_all = from_root(leaving, "lon", anchor)
    return prefix + factor * beside_all / closure


def band_carry(edge_sums, inverse_level, length, reverse):
    inverse = jnp.transpose(inverse_level, (2, 0, 1))[..., None]
    stride = jnp.exp(-length * inverse)
    factor, prefix = prefix_2(
        (stride, edge_sums),
        "lat",
        affine_join,
        (jnp.ones_like(stride), jnp.zeros_like(edge_sums)),
        reverse,
    )
    return prefix


def lon_pass(current, blocks, inverse, weights, level_group, reverse):
    cells = current.shape[3]
    position = jnp.arange(cells).astype(jnp.float32)
    if reverse:
        edge_gap = position
        inward = cells - position
        pattern = "vkaj,vij->vkai"
    else:
        edge_gap = cells - 1.0 - position
        inward = position + 1.0
        pattern = "vkaj,vji->vkai"
    edge_weight = jnp.exp(-edge_gap * inverse[..., None])
    edge_sums = jnp.einsum("vkal,vkpl->pvka", current, edge_weight, precision=lax.Precision.HIGHEST)
    inside = grouped_product(current, blocks, level_group, pattern)
    incoming = cycle_carry(edge_sums, inverse, cells, reverse)
    decay = weights[..., None] * jnp.exp(-inward * inverse[..., None])
    return inside + jnp.einsum("pvka,vkpl->vkal", incoming, decay, precision=lax.Precision.HIGHEST)


def lat_pass(current, blocks, inverse, weights, level_group, reverse):
    height = current.shape[2]
    position = jnp.arange(height).astype(jnp.float32)
    if reverse:
        edge_gap = position
        inward = height - position
        pattern = "vkjl,vij->vkil"
    else:
        edge_gap = height - 1.0 - position
        inward = position + 1.0
        pattern = "vkjl,vji->vkil"
    edge_weight = jnp.exp(-edge_gap * inverse[..., None])
    edge_sums = jnp.einsum("vkal,vkpa->pvkl", current, edge_weight, precision=lax.Precision.HIGHEST)
    inside = grouped_product(current, blocks, level_group, pattern)
    incoming = band_carry(edge_sums, inverse, height, reverse)
    decay = weights[..., None] * jnp.exp(-inward * inverse[..., None])
    return inside + jnp.einsum("pvkl,vkpa->vkal", incoming, decay, precision=lax.Precision.HIGHEST)


def per_device(
    increment, std_dev, level_group, lon_reach, lon_weight, lat_reach, lat_weight, vertical
):
    height = increment.shape[2]
    cells = increment.shape[3]
    groups = lon_reach.shape[1]
    onehot = (level_group[:, None] == jnp.arange(groups, dtype=jnp.int32)[None, :]).astype(
        jnp.float32
    )
    inverse_lon_group = 1.0 / lon_reach
    weights_lon_group = lon_weight * (1.0 - jnp.exp(-inverse_lon_group))
    inverse_lat_group = 1.0 / lat_reach
    weights_lat_group = lat_weight * (1.0 - jnp.exp(-inverse_lat_group))
    inverse_lon = level_values(onehot, inverse_lon_group)
    inverse_lat = level_values(onehot, inverse_lat_group)
    weights_lat = level_values(onehot, weights_lat_group)
    blocks_lat = toeplitz_tables(inverse_lat_group, weights_lat_group, height)
    spread_dev = std_dev.astype(jnp.float32)
    current = spread_dev * increment.astype(jnp.float32)
    weights_lon = level_values(onehot, weights_lon_group)
    blocks_lon = toeplitz_tables(inverse_lon_group, weights_lon_group, cells)
    current = lon_pass(current, blocks_lon, inverse_lon, weights_lon, level_group, False)
    current = lon_pass(current, blocks_lon, inverse_lon, weights_lon, level_group, True)
    current = lat_pass(current, blocks_lat, inverse_lat, weights_lat, level_group, False)
    current = lat_pass(current, blocks_lat, inverse_lat, weights_lat, level_group, True)
    mixed = jnp.einsum("vkj,vjal->vkal", vertical, current, precision=lax.Precision.HIGHEST)
    return (spread_dev * mixed).astype(jnp.bfloat16)


def solution(mesh):
    placed = (
        P(None, None, "lat", "lon"),
        P(None, None, "lat", "lon"),
        P(),
        P(),
        P(),
        P(),
        P(),
        P(),
    )
    return jax.shard_map(
        per_device,
        mesh=mesh,
        in_specs=placed,
        out_specs=P(None, None, "lat", "lon"),
        check_vma=False,
    )
```

profile of v0, /device:TPU:2, one launch (start us, length us, event | category | flops | bytes accessed | tf_op | source)
XLA Modules:
  0.0 1333.2 jit_solution(13357171241874565079)
XLA Ops:
  6.5 1.5 fusion.120
  15.0 1.5 convolution_bitcast_fusion.5
  16.5 1.4 multiply_reduce_fusion
  18.6 1.4 convert_multiply_fusion.1
  20.0 1.9 convolution_bitcast_fusion.3
  22.1 122.4 %all-gather.1 = f32[128,2,127,8]{2,3,1,0:T(8,128)S(1)} all-gather(f32[4,2,127,8]{2,3,1,0:T(8,128)S(1)} %copy.93), channel_id=3, replica_groups=mesh['lon'=32,'lat'=16] {'lon'}, dimensions={0}, use_global_device_ids=true | all-gather | bytes 1072896 | tf_op jit(solution)/shard_map/all_gather | solution.py:13
  144.5 102.7 %all-gather = f32[128,2,127]{2,1,0:T(2,128)S(1)} all-gather(f32[4,2,127]{2,1,0:T(2,128)S(1)} %copy.91), channel_id=2, replica_groups=mesh['lon'=32,'lat'=16] {'lon'}, dimensions={0}, use_global_device_ids=true | all-gather | bytes 134112 | tf_op jit(solution)/shard_map/all_gather | solution.py:13
  248.7 226.5 %psum.14 = f32[4,2,127,8]{3,0,2,1:T(4,128)S(1)} all-reduce(f32[4,2,127,8]{3,0,2,1:T(4,128)S(1)} %add_select_fusion.1), channel_id=1, replica_groups=mesh['lon'=32,'lat'=16] {'lon'}, use_global_device_ids=true, to_apply=%region_8.9 | all-reduce | flops 8128 | bytes 65024 | tf_op jit(solution)/shard_map/psum | solution.py:27
  481.0 2.8 convolution_add_fusion.3
  484.8 1.9 convolution_bitcast_fusion.2
  486.9 119.1 %all-gather.2 = f32[128,2,127,8]{2,3,1,0:T(8,128)S(1)} all-gather(f32[4,2,127,8]{2,3,1,0:T(8,128)S(1)} %copy.105), channel_id=4, replica_groups=mesh['lon'=32,'lat'=16] {'lon'}, dimensions={0}, use_global_device_ids=true | all-gather | bytes 1072896 | tf_op jit(solution)/shard_map/all_gather | solution.py:13
  606.0 32.0 %while.53 = (s32[]{:T(128)}, f32[4,2,127,1]{2,3,1,0:T(1,128)S(1)}, f32[4,2,127,8]{2,3,1,0:T(8,128)S(1)}, s32[]{:T(128)}, f32[32,4,2,127,1]{3,2,1,4,0:T(2,128)}, ...) while((s32[]{:T(128)}, f32[4,2,127,1]{2,3,1,0:T(1,128)S(1)}, ...), condition=%wide.region_10.11_spmd, body=%wide.region_9.10_spmd.sunk | while | flops 17278 | bytes 130207 | solution.py:22
  638.4 245.2 %psum.15 = f32[4,2,127,8]{3,0,2,1:T(4,128)S(1)} all-reduce(f32[4,2,127,8]{3,0,2,1:T(4,128)S(1)} %add_select_fusion), channel_id=1, replica_groups=mesh['lon'=32,'lat'=16] {'lon'}, use_global_device_ids=true, to_apply=%region_11.12 | all-reduce | flops 8128 | bytes 65024 | tf_op jit(solution)/shard_map/psum | solution.py:27
  885.7 1.4 fusion.24
  887.1 1.4 fusion.33
  890.0 3.9 convolution_add_fusion.2
  894.0 1.9 convolution_bitcast_fusion.1
  898.1 42.6 %all-gather.3 = f32[64,2,127]{2,1,0:T(2,128)S(1)} all-gather(f32[4,2,127]{2,1,0:T(2,128)S(1)} %copy.121), channel_id=5, replica_groups=mesh['lon'=32,'lat'=16] {'lat'}, dimensions={0}, use_global_device_ids=true | all-gather | bytes 69088 | tf_op jit(solution)/shard_map/all_gather | solution.py:13
  942.9 159.9 %all-gather.9.cloned.1.call-done = f32[64,2,127,128]{3,1,2,0:T(2,128)} async-done(((f32[4,2,127,128]{3,1,2,0:T(2,128)}), f32[64,2,127,128]{3,1,2,0:T(2,128)}) %all-gather.9.cloned.1.call-update) | async-done | bytes 8323088 | tf_op jit(solution)/shard_map/all_gather | solution.py:13
  1103.8 4.0 convolution_add_fusion.1
  1107.7 1.9 convolution_bitcast_fusion
  1112.6 186.0 %all-gather.11.cloned.1.call-done = f32[64,2,127,128]{3,1,2,0:T(2,128)} async-done(((f32[4,2,127,128]{3,1,2,0:T(2,128)}), f32[64,2,127,128]{3,1,2,0:T(2,128)}) %all-gather.11.cloned.1.call-update) | async-done | bytes 8323088 | tf_op jit(solution)/shard_map/all_gather | solution.py:13
  1298.6 21.4 %while.55 = (s32[]{:T(128)}, f32[4,2,127,128]{3,2,1,0:T(8,128)S(1)}, s32[]{:T(128)}, f32[16,4,2,127,1]{3,2,1,4,0:T(2,128)S(1)}, f32[16,4,2,127,128]{4,2,3,1,0:T(...) while((s32[]{:T(128)}, f32[4,2,127,128]{3,2,1,0:T(8,128)S(1)}, s32[]{:T(128)}, ...), condition=%wide.region_15.16_spmd, body=%wide.region_14.15_spmd.sunk | while | flops 260102 | bytes 2613299 | solution.py:22
  1298.6 1.1 constant_dynamic-slice_fusion.11
  1300.1 1.1 constant_dynamic-slice_fusion.11
  1301.5 1.1 constant_dynamic-slice_fusion.11
  1304.3 1.1 constant_dynamic-slice_fusion.11
  1307.1 1.1 constant_dynamic-slice_fusion.11
  1314.1 1.1 constant_dynamic-slice_fusion.11
  1317.0 1.1 constant_dynamic-slice_fusion.11
  1320.0 3.0 convolution_add_fusion
  1323.0 1.8 fusion.38
  (300 shorter events, 72.1 us)
Async XLA Ops:
  6.5 1316.4 %copy-start = (f32[2,127,127]{2,0,1:T(2,128)S(1)}, f32[2,127,127]{2,0,1:T(2,128)}, u32[]{:S(2)}) copy-start(f32[2,127,127]{2,0,1:T(2,128)} %param.23) | copy-start | bytes 387100
  6.5 13.4 %copy-start.5 = (bf16[2,127,8,128]{3,2,1,0:T(8,128)(2,1)S(1)}, bf16[2,127,8,128]{3,2,1,0:T(8,128)(2,1)}, u32[]{:S(2)}) copy-start(bf16[2,127,8,128]{3,2,1,0:T(8,128)(2,1)} %param.16) | copy-start | bytes 1560580
  6.5 13.4 %copy-start.1 = (bf16[2,127,8,128]{3,2,1,0:T(8,128)(2,1)S(1)}, bf16[2,127,8,128]{3,2,1,0:T(8,128)(2,1)}, u32[]{:S(2)}) copy-start(bf16[2,127,8,128]{3,2,1,0:T(8,128)(2,1)} %param.17) | copy-start | bytes 1560580
  6.5 1096.3 %all-gather.9.cloned.1.call-start = ((), (), s32[]{:S(2)}) async-start(), calls=%async_computation | async-start | bytes 8843264 | tf_op jit(solution)/shard_map/all_gather | solution.py:13
  18.6 1.4 copy-start.7
  144.5 330.6 %copy-start.13 = (f32[4,2,127]{2,1,0:T(2,128)}, f32[4,2,127]{2,1,0:T(2,128)S(1)}, u32[]{:S(2)}) copy-start(f32[4,2,127]{2,1,0:T(2,128)S(1)} %copy.91) | copy-start | bytes 12196
  248.0 0.6 copy-start.6
  475.2 3.0 copy-start.4
  475.2 3.8 copy-start.15
  478.1 2.9 copy-start.12
  479.0 406.6 %copy-start.20 = (pred[40]{0:T(512)(128)(4,1)}, pred[40]{0:T(512)(128)(4,1)S(1)}, u32[]{:S(2)}) copy-start(pred[40]{0:T(512)(128)(4,1)S(1)} %get-tuple-element.377) | copy-start | bytes 124
  479.0 408.1 %copy-start.18 = (pred[40]{0:T(512)(128)(4,1)}, pred[40]{0:T(512)(128)(4,1)S(1)}, u32[]{:S(2)}) copy-start(pred[40]{0:T(512)(128)(4,1)S(1)} %get-tuple-element.376) | copy-start | bytes 124
  479.1 409.6 %copy-start.16 = (pred[40]{0:T(512)(128)(4,1)}, pred[40]{0:T(512)(128)(4,1)S(1)}, u32[]{:S(2)}) copy-start(pred[40]{0:T(512)(128)(4,1)S(1)} %get-tuple-element.375) | copy-start | bytes 124
  479.1 1.8 copy-start.8
  479.2 1.8 copy-start.27
  481.0 3.8 copy-start.26
  483.8 1.0 copy-start.2
  484.8 153.1 %copy-start.14 = (f32[4,2,127]{2,1,0:T(2,128)S(1)}, f32[4,2,127]{2,1,0:T(2,128)}, u32[]{:S(2)}) copy-start(f32[4,2,127]{2,1,0:T(2,128)} %copy-done.13) | copy-start | bytes 12196
  884.6 4.1 copy-start.3
  885.7 3.9 copy-start.22
  885.7 3.9 copy-start.23
  885.7 4.3 copy-start.25
  889.6 4.3 copy-start.24
  890.0 5.9 copy-start.9
  893.9 47.0 %copy-start.21 = (pred[40]{0:T(512)(128)(4,1)S(1)}, pred[40]{0:T(512)(128)(4,1)}, u32[]{:S(2)}) copy-start(pred[40]{0:T(512)(128)(4,1)} %copy-done.20) | copy-start | bytes 124
  895.9 45.5 %copy-start.19 = (pred[40]{0:T(512)(128)(4,1)S(1)}, pred[40]{0:T(512)(128)(4,1)}, u32[]{:S(2)}) copy-start(pred[40]{0:T(512)(128)(4,1)} %copy-done.18) | copy-start | bytes 124
  895.9 46.0 %copy-start.17 = (pred[40]{0:T(512)(128)(4,1)S(1)}, pred[40]{0:T(512)(128)(4,1)}, u32[]{:S(2)}) copy-start(pred[40]{0:T(512)(128)(4,1)} %copy-done.16) | copy-start | bytes 124
  897.0 401.6 %all-gather.11.cloned.1.call-start = ((), (), s32[]{:S(2)}) async-start(), calls=%async_computation.1 | async-start | bytes 8843264 | tf_op jit(solution)/shard_map/all_gather | solution.py:13
  1102.9 0.9 copy-start.10
  1298.6 21.4 %copy-start.11 = (f32[2,127,4]{2,1,0:T(8,128)S(1)}, f32[2,127,4]{2,1,0:T(8,128)}, u32[]{:S(2)}) copy-start(f32[2,127,4]{2,1,0:T(8,128)} %copy.118) | copy-start | bytes 12196
Sparse Core Ops, SparseCore 0:
  897.1 205.6 all-gather.8
  1110.9 187.6 all-gather.10
where the time goes:
time: 1340 us; the launch traced here: 1330 us
  blocking collectives  858 us (64%)
  waiting for transfers between devices  346 us (26%)
  local copies, waits for them, and re-layouts  58.4 us (4%)
  matrix products  35.1 us (3%)
  between operations  17 us (1%)
  other arithmetic  16.9 us (1%)
    psum x2, blocking collectives, from_root(): return lax.psum(kept, axis)  472 us
    all_gather x4, blocking collectives, prefix_2(): gathered = jax.tree.map(lambda a: lax.all_gather(a, axis), part)  387 us
    all_gather x2, waiting for transfers between devices, prefix_2(): gathered = jax.tree.map(lambda a: lax.all_gather(a, axis), part)  346 us
    dynamic_slice x46, local copies, waits for them, and re-layouts, one(): lax.dynamic_index_in_dim(a, source, 0, False)  32 us
  transfers between devices with their start and end apart: 2, of which 2 were waited for; matrix products, arithmetic and copies ran while one was open for 0% of the time, Pallas kernels for 0%

commit v1 on v0

--- a/solution.py
+++ b/solution.py
@@ -24,7 +24,7 @@
 
 def from_root(value, axis, source):
     kept = jnp.where(lax.axis_index(axis) == source, value, 0).astype(value.dtype)
-    return lax.psum(kept, axis)
+    return jnp.sum(lax.all_gather(kept, axis), axis=0)
 
 
 def level_values(onehot, grouped):

time: 1340 us -> 1120 us (0.84)
  blocking collectives: 858 us -> 638 us
    psum x2 -> x0, blocking collectives: 472 us -> none  [from_root(): return lax.psum(kept, axis)]
    all_gather x0 -> x2, blocking collectives: none -> 250 us  [from_root(): return jnp.sum(lax.all_gather(kept, axis), axis=0)]
where the time goes in v1:
time: 1120 us; the launch traced here: 1110 us
  blocking collectives  638 us (57%)
  waiting for transfers between devices  344 us (31%)
  local copies, waits for them, and re-layouts  59.1 us (5%)
  matrix products  35.1 us (3%)
  other arithmetic  17.1 us (2%)
  between operations  16.9 us (2%)
    all_gather x4, blocking collectives, prefix_2(): gathered = jax.tree.map(lambda a: lax.all_gather(a, axis), part)  388 us
    all_gather x2, waiting for transfers between devices, prefix_2(): gathered = jax.tree.map(lambda a: lax.all_gather(a, axis), part)  344 us
    all_gather x2, blocking collectives, from_root(): return jnp.sum(lax.all_gather(kept, axis), axis=0)  250 us
    dynamic_slice x46, local copies, waits for them, and re-layouts, one(): lax.dynamic_index_in_dim(a, source, 0, False)  32 us
  transfers between devices with their start and end apart: 2, of which 2 were waited for; matrix products, arithmetic and copies ran while one was open for 0% of the time, Pallas kernels for 0%

profile of v1, /device:TPU:2, one launch (start us, length us, event | category | flops | bytes accessed | tf_op | source)
XLA Modules:
  0.0 1111.8 jit_solution(6695777908733800528)
XLA Ops:
  6.5 1.5 fusion.120
  15.0 1.5 convolution_bitcast_fusion.5
  16.5 1.4 multiply_reduce_fusion
  18.6 1.4 convert_multiply_fusion.1
  20.0 1.9 convolution_bitcast_fusion.3
  22.1 122.4 %all-gather.1 = f32[128,2,127,8]{2,3,1,0:T(8,128)S(1)} all-gather(f32[4,2,127,8]{2,3,1,0:T(8,128)S(1)} %copy.93), channel_id=3, replica_groups=mesh['lon'=32,'lat'=16] {'lon'}, dimensions={0}, use_global_device_ids=true | all-gather | bytes 1072896 | tf_op jit(solution)/shard_map/all_gather | solution.py:13
  144.5 102.6 %all-gather = f32[128,2,127]{2,1,0:T(2,128)S(1)} all-gather(f32[4,2,127]{2,1,0:T(2,128)S(1)} %copy.91), channel_id=2, replica_groups=mesh['lon'=32,'lat'=16] {'lon'}, dimensions={0}, use_global_device_ids=true | all-gather | bytes 134112 | tf_op jit(solution)/shard_map/all_gather | solution.py:13
  248.6 114.7 %all-gather.2 = f32[128,2,127,8]{2,3,1,0:T(8,128)S(1)} all-gather(f32[4,2,127,8]{2,3,1,0:T(8,128)S(1)} %copy.100), channel_id=4, replica_groups=mesh['lon'=32,'lat'=16] {'lon'}, dimensions={0}, use_global_device_ids=true | all-gather | bytes 1072896 | tf_op jit(solution)/shard_map/all_gather | solution.py:27
  369.4 2.8 convolution_add_fusion.3
  373.2 1.9 convolution_bitcast_fusion.2
  375.3 120.9 %all-gather.3 = f32[128,2,127,8]{2,3,1,0:T(8,128)S(1)} all-gather(f32[4,2,127,8]{2,3,1,0:T(8,128)S(1)} %copy.107), channel_id=5, replica_groups=mesh['lon'=32,'lat'=16] {'lon'}, dimensions={0}, use_global_device_ids=true | all-gather | bytes 1072896 | tf_op jit(solution)/shard_map/all_gather | solution.py:13
  496.2 32.0 %while.53 = (s32[]{:T(128)}, f32[4,2,127,1]{2,3,1,0:T(1,128)S(1)}, f32[4,2,127,8]{2,3,1,0:T(8,128)S(1)}, s32[]{:T(128)}, f32[32,4,2,127,1]{3,2,1,4,0:T(2,128)}, ...) while((s32[]{:T(128)}, f32[4,2,127,1]{2,3,1,0:T(1,128)S(1)}, ...), condition=%wide.region_10.11_spmd, body=%wide.region_9.10_spmd.sunk | while | flops 17278 | bytes 130207 | solution.py:22
  528.9 135.1 %all-gather.4 = f32[128,2,127,8]{2,3,1,0:T(8,128)S(1)} all-gather(f32[4,2,127,8]{2,3,1,0:T(8,128)S(1)} %copy.113), channel_id=6, replica_groups=mesh['lon'=32,'lat'=16] {'lon'}, dimensions={0}, use_global_device_ids=true | all-gather | bytes 1072896 | tf_op jit(solution)/shard_map/all_gather | solution.py:27
  666.4 1.4 fusion.24
  667.9 1.5 fusion.33
  670.7 3.9 convolution_add_fusion.2
  674.7 1.9 convolution_bitcast_fusion.1
  678.8 42.1 %all-gather.5 = f32[64,2,127]{2,1,0:T(2,128)S(1)} all-gather(f32[4,2,127]{2,1,0:T(2,128)S(1)} %copy.125), channel_id=7, replica_groups=mesh['lon'=32,'lat'=16] {'lat'}, dimensions={0}, use_global_device_ids=true | all-gather | bytes 69088 | tf_op jit(solution)/shard_map/all_gather | solution.py:13
  723.1 158.2 %all-gather.11.cloned.1.call-done = f32[64,2,127,128]{3,1,2,0:T(2,128)} async-done(((f32[4,2,127,128]{3,1,2,0:T(2,128)}), f32[64,2,127,128]{3,1,2,0:T(2,128)}) %all-gather.11.cloned.1.call-update) | async-done | bytes 8323088 | tf_op jit(solution)/shard_map/all_gather | solution.py:13
  882.3 4.0 convolution_add_fusion.1
  886.3 1.9 convolution_bitcast_fusion
  891.1 186.0 %all-gather.13.cloned.1.call-done = f32[64,2,127,128]{3,1,2,0:T(2,128)} async-done(((f32[4,2,127,128]{3,1,2,0:T(2,128)}), f32[64,2,127,128]{3,1,2,0:T(2,128)}) %all-gather.13.cloned.1.call-update) | async-done | bytes 8323088 | tf_op jit(solution)/shard_map/all_gather | solution.py:13
  1077.1 21.4 %while.55 = (s32[]{:T(128)}, f32[4,2,127,128]{3,2,1,0:T(8,128)S(1)}, s32[]{:T(128)}, f32[16,4,2,127,1]{3,2,1,4,0:T(2,128)S(1)}, f32[16,4,2,127,128]{4,2,3,1,0:T(...) while((s32[]{:T(128)}, f32[4,2,127,128]{3,2,1,0:T(8,128)S(1)}, s32[]{:T(128)}, ...), condition=%wide.region_15.16_spmd, body=%wide.region_14.15_spmd.sunk | while | flops 260102 | bytes 2613299 | solution.py:22
  1077.2 1.1 constant_dynamic-slice_fusion.11
  1078.6 1.1 constant_dynamic-slice_fusion.11
  1080.0 1.1 constant_dynamic-slice_fusion.11
  1087.0 1.1 constant_dynamic-slice_fusion.11
  1089.9 1.1 constant_dynamic-slice_fusion.11
  1094.1 1.1 constant_dynamic-slice_fusion.11
  1096.9 1.1 constant_dynamic-slice_fusion.11
  1098.5 3.0 convolution_add_fusion
  1101.5 1.8 fusion.38
  (306 shorter events, 73.0 us)
Async XLA Ops:
  6.5 1095.0 %copy-start = (f32[2,127,127]{2,0,1:T(2,128)S(1)}, f32[2,127,127]{2,0,1:T(2,128)}, u32[]{:S(2)}) copy-start(f32[2,127,127]{2,0,1:T(2,128)} %param.23) | copy-start | bytes 387100
  6.5 13.4 %copy-start.5 = (bf16[2,127,8,128]{3,2,1,0:T(8,128)(2,1)S(1)}, bf16[2,127,8,128]{3,2,1,0:T(8,128)(2,1)}, u32[]{:S(2)}) copy-start(bf16[2,127,8,128]{3,2,1,0:T(8,128)(2,1)} %param.16) | copy-start | bytes 1560580
  6.5 13.4 %copy-start.1 = (bf16[2,127,8,128]{3,2,1,0:T(8,128)(2,1)S(1)}, bf16[2,127,8,128]{3,2,1,0:T(8,128)(2,1)}, u32[]{:S(2)}) copy-start(bf16[2,127,8,128]{3,2,1,0:T(8,128)(2,1)} %param.17) | copy-start | bytes 1560580
  6.5 874.8 %all-gather.11.cloned.1.call-start = ((), (), s32[]{:S(2)}) async-start(), calls=%async_computation | async-start | bytes 8843264 | tf_op jit(solution)/shard_map/all_gather | solution.py:13
  18.6 1.4 copy-start.7
  144.5 218.7 %copy-start.13 = (f32[4,2,127]{2,1,0:T(2,128)}, f32[4,2,127]{2,1,0:T(2,128)S(1)}, u32[]{:S(2)}) copy-start(f32[4,2,127]{2,1,0:T(2,128)S(1)} %copy.91) | copy-start | bytes 12196
  247.9 115.4 %copy-start.6 = (f32[32,4,2,127,1]{3,2,1,4,0:T(2,128)}, f32[32,4,2,127,1]{3,2,1,4,0:T(2,128)S(1)}, u32[]{:S(2)}) copy-start(f32[32,4,2,127,1]{3,2,1,4,0:T(2,128)S(1)} %get-tuple-element.634) | copy-start | bytes 390148
  363.3 3.3 copy-start.4
  363.6 3.8 copy-start.15
  366.5 2.9 copy-start.12
  367.5 298.9 %copy-start.20 = (pred[40]{0:T(512)(128)(4,1)}, pred[40]{0:T(512)(128)(4,1)S(1)}, u32[]{:S(2)}) copy-start(pred[40]{0:T(512)(128)(4,1)S(1)} %get-tuple-element.377) | copy-start | bytes 124
  367.5 300.4 %copy-start.18 = (pred[40]{0:T(512)(128)(4,1)}, pred[40]{0:T(512)(128)(4,1)S(1)}, u32[]{:S(2)}) copy-start(pred[40]{0:T(512)(128)(4,1)S(1)} %get-tuple-element.376) | copy-start | bytes 124
  367.5 301.8 %copy-start.16 = (pred[40]{0:T(512)(128)(4,1)}, pred[40]{0:T(512)(128)(4,1)S(1)}, u32[]{:S(2)}) copy-start(pred[40]{0:T(512)(128)(4,1)S(1)} %get-tuple-element.375) | copy-start | bytes 124
  367.6 1.8 copy-start.8
  367.6 1.8 copy-start.27
  369.4 3.8 copy-start.26
  372.3 1.0 copy-start.2
  373.2 155.0 %copy-start.14 = (f32[4,2,127]{2,1,0:T(2,128)S(1)}, f32[4,2,127]{2,1,0:T(2,128)}, u32[]{:S(2)}) copy-start(f32[4,2,127]{2,1,0:T(2,128)} %copy-done.13) | copy-start | bytes 12196
  665.3 4.1 copy-start.3
  666.4 3.9 copy-start.22
  666.4 3.9 copy-start.23
  666.4 4.3 copy-start.25
  670.3 4.4 copy-start.24
  670.7 5.9 copy-start.9
  674.7 46.4 %copy-start.21 = (pred[40]{0:T(512)(128)(4,1)S(1)}, pred[40]{0:T(512)(128)(4,1)}, u32[]{:S(2)}) copy-start(pred[40]{0:T(512)(128)(4,1)} %copy-done.20) | copy-start | bytes 124
  676.6 45.0 %copy-start.19 = (pred[40]{0:T(512)(128)(4,1)S(1)}, pred[40]{0:T(512)(128)(4,1)}, u32[]{:S(2)}) copy-start(pred[40]{0:T(512)(128)(4,1)} %copy-done.18) | copy-start | bytes 124
  676.6 45.5 %copy-start.17 = (pred[40]{0:T(512)(128)(4,1)S(1)}, pred[40]{0:T(512)(128)(4,1)}, u32[]{:S(2)}) copy-start(pred[40]{0:T(512)(128)(4,1)} %copy-done.16) | copy-start | bytes 124
  677.7 399.4 %all-gather.13.cloned.1.call-start = ((), (), s32[]{:S(2)}) async-start(), calls=%async_computation.1 | async-start | bytes 8843264 | tf_op jit(solution)/shard_map/all_gather | solution.py:13
  881.4 0.9 copy-start.10
  1077.1 21.4 %copy-start.11 = (f32[2,127,4]{2,1,0:T(8,128)S(1)}, f32[2,127,4]{2,1,0:T(8,128)}, u32[]{:S(2)}) copy-start(f32[2,127,4]{2,1,0:T(8,128)} %copy.122) | copy-start | bytes 12196
Sparse Core Ops, SparseCore 0:
  677.8 203.5 all-gather.10
  889.4 187.6 all-gather.12
